TPU v7x, 128 devices: a whole 4x4x4 slice. The times are simulated.
128 devices in a mesh: lon: 16 (over x, y_lo, core), lat: 8 (over z, y_hi).
Axes of the slice: x: 4, y: 4 (y_hi: 2, y_lo: 2; y = y_hi * 2 + y_lo), z: 4, core: 2. Of those that a mesh axis runs over, the one named last changes fastest.
Arguments:
- heat_content_field: float32 [12, 768, 2048], P(None, 'lat', 'lon'), may hold values from -6 to 6
- saltiness_field: float32 [12, 768, 2048], P(None, 'lat', 'lon'), may hold values from -6 to 6
- eastward_cfl_number: float32 [12, 768, 2048], P(None, 'lat', 'lon'), may hold values from -0.4 to 0.4
- northward_cfl_number: float32 [12, 768, 2048], P(None, 'lat', 'lon'), may hold values from -0.4 to 0.4
- seawater_indicator: int32 [768, 2048], P('lat', 'lon'), may hold values 0 or 1
- submerged_layer_total: int32 [768, 2048], P('lat', 'lon'), may hold values from 1 to 12
- seam_partner_index: int32 [2048], replicated, may hold values from 0 to 2047, as said below
Outputs:
- new_temperature: float32 [12, 768, 2048], P(None, 'lat', 'lon')
- new_salinity: float32 [12, 768, 2048], P(None, 'lat', 'lon')
Inputs may be any that keep to these rules, and one draw needn't show every extreme that they name: Each column appears once; the map is a reflection of the columns about a pivot, seam_partner_index[i] = (s - i) mod 2048.
All inputs are finite; a program needn't handle non-finite values. No bound on the sum of `seawater_indicator` on one device may be relied on, other than what follows from the above.
Results may differ from a plain program's by a relative error of at most 0.0003.
Values sent between devices are 32-bit elements; how exact they have to be, the bound alone decides.
A program may use at most 192 MiB of HBM per device.

v0:
```python
from functools import reduce
import jax
import jax.numpy as jnp
from jax import lax
from jax.sharding import PartitionSpec as P

RATIO_FLOOR = 0.05
SLOPE_FLOOR = 0.5
SLOPE_LIMIT = 2.0
DIFFUSIVITY = 0.1
THERMAL_COEF = 0.2
HALINE_COEF = 0.8
STATE_SIGNS = (1.0, 1.0, -1.0, -1.0, 1.0)


def extended(cells, sides, width, closed):
    for axis, dim in sides:
        count = lax.axis_size(axis)
        ends = count if closed else count - 1
        head = lax.slice_in_dim(cells, 0, width, axis=dim)
        tail = lax.slice_in_dim(cells, cells.shape[dim] - width, cells.shape[dim], axis=dim)
        cells = jnp.concatenate(
            [
                lax.ppermute(tail, axis, [(i, (i + 1) % count) for i in range(ends)]),
                cells,
                lax.ppermute(head, axis, [((i + 1) % count, i) for i in range(ends)]),
            ],
            axis=dim,
        )
    return cells


def sign_column(values):
    return jnp.array(values, jnp.float32).reshape(len(values), 1, 1, 1)


def sided(core, west_col, east_col, south_row, north_row):
    width = core.shape[-1]
    height = core.shape[-2]
    lane = lax.broadcasted_iota(jnp.int32, core.shape, core.ndim - 1)
    level = lax.broadcasted_iota(jnp.int32, core.shape, core.ndim - 2)
    at_east = jnp.where(lane == width - 1, east_col, jnp.roll(core, -1, axis=-1))
    at_west = jnp.where(lane == 0, west_col, jnp.roll(core, 1, axis=-1))
    at_north = jnp.where(level == height - 1, north_row, jnp.roll(core, -1, axis=-2))
    at_south = jnp.where(level == 0, south_row, jnp.roll(core, 1, axis=-2))
    return (core, at_east, at_west, at_north, at_south)


def low_order(tracer, zonal, meridional, wet_sides):
    value_centre, value_east, value_west, value_north, value_south = tracer
    speed_centre, speed_west = (zonal[0], zonal[2])
    flow_centre, flow_south = (meridional[0], meridional[4])
    wet_centre, wet_east, wet_west, wet_north, wet_south = wet_sides
    face_east = wet_centre * wet_east
    face_west = wet_west * wet_centre
    face_north = wet_centre * wet_north
    face_south = wet_south * wet_centre
    upwind_east = face_east * (
        jnp.maximum(speed_centre, 0.0) * value_centre + jnp.minimum(speed_centre, 0.0) * value_east
    )
    upwind_west = face_west * (
        jnp.maximum(speed_west, 0.0) * value_west + jnp.minimum(speed_west, 0.0) * value_centre
    )
    upwind_north = face_north * (
        jnp.maximum(flow_centre, 0.0) * value_centre + jnp.minimum(flow_centre, 0.0) * value_north
    )
    upwind_south = face_south * (
        jnp.maximum(flow_south, 0.0) * value_south + jnp.minimum(flow_south, 0.0) * value_centre
    )
    anti_east = face_east * speed_centre * (value_centre + value_east) * 0.5 - upwind_east
    anti_west = face_west * speed_west * (value_west + value_centre) * 0.5 - upwind_west
    anti_north = face_north * flow_centre * (value_centre + value_north) * 0.5 - upwind_north
    anti_south = face_south * flow_south * (value_south + value_centre) * 0.5 - upwind_south
    upwind = value_centre - wet_centre * (upwind_east - upwind_west + upwind_north - upwind_south)
    inflow = (
        jnp.maximum(anti_west, 0.0)
        - jnp.minimum(anti_east, 0.0)
        + jnp.maximum(anti_south, 0.0)
        - jnp.minimum(anti_north, 0.0)
    )
    outflow = (
        jnp.maximum(anti_east, 0.0)
        - jnp.minimum(anti_west, 0.0)
        + jnp.maximum(anti_north, 0.0)
        - jnp.minimum(anti_south, 0.0)
    )
    anti = (anti_east, anti_west, anti_north, anti_south)
    return (upwind, anti, inflow, outflow)


def ratios(upwind_sides, wet_sides, inflow, outflow):
    value_centre, value_east, value_west, value_north, value_south = upwind_sides
    _, wet_east, wet_west, wet_north, wet_south = wet_sides
    pairs = (
        (value_east, wet_east),
        (value_west, wet_west),
        (value_north, wet_north),
        (value_south, wet_south),
    )
    candidates = [value_centre] + [
        jnp.where(beside_wet > 0.5, beside, value_centre) for beside, beside_wet in pairs
    ]
    highest = reduce(jnp.maximum, candidates)
    lowest = reduce(jnp.minimum, candidates)
    ratio_plus = jnp.minimum(1.0, (highest - value_centre) / jnp.maximum(inflow, RATIO_FLOOR))
    ratio_minus = jnp.minimum(1.0, (value_centre - lowest) / jnp.maximum(outflow, RATIO_FLOOR))
    return jnp.concatenate([ratio_plus, ratio_minus], axis=0)


def limited(ratio_sides, upwind, anti, wet_centre):
    plus_centre, plus_east, plus_west, plus_north, plus_south = [side[:2] for side in ratio_sides]
    minus_centre, minus_east, minus_west, minus_north, minus_south = [
        side[2:] for side in ratio_sides
    ]
    anti_east, anti_west, anti_north, anti_south = anti
    coef_east = jnp.where(
        anti_east >= 0.0, jnp.minimum(plus_east, minus_centre), jnp.minimum(plus_centre, minus_east)
    )
    coef_west = jnp.where(
        anti_west >= 0.0, jnp.minimum(plus_centre, minus_west), jnp.minimum(plus_west, minus_centre)
    )
    coef_north = jnp.where(
        anti_north >= 0.0,
        jnp.minimum(plus_north, minus_centre),
        jnp.minimum(plus_centre, minus_north),
    )
    coef_south = jnp.where(
        anti_south >= 0.0,
        jnp.minimum(plus_centre, minus_south),
        jnp.minimum(plus_south, minus_centre),
    )
    return upwind - wet_centre * (
        coef_east * anti_east
        - coef_west * anti_west
        + coef_north * anti_north
        - coef_south * anti_south
    )


def vertical_of(tracer, wet):
    stacked_wet = wet[:-1] * wet[1:]
    vertical = (tracer[:, 1:] - tracer[:, :-1]) * stacked_wet
    return jnp.concatenate([vertical, jnp.zeros_like(tracer[:, :1])], axis=1)


def isopycnal(values, wet_sides):
    verticals = tuple((vertical_of(tracer, wet) for tracer, wet in zip(values, wet_sides)))
    densities = tuple((HALINE_COEF * tracer[1] - THERMAL_COEF * tracer[0] for tracer in values))
    stratas = tuple(
        (HALINE_COEF * vertical[1] - THERMAL_COEF * vertical[0] for vertical in verticals)
    )

    def face_flux(first, second):
        face = wet_sides[first] * wet_sides[second]
        slope = jnp.clip(
            (densities[second] - densities[first])
            / jnp.maximum(0.5 * (stratas[first] + stratas[second]), SLOPE_FLOOR),
            -SLOPE_LIMIT,
            SLOPE_LIMIT,
        )
        return (
            DIFFUSIVITY
            * face
            * (
                values[second]
                - values[first]
                - slope * 0.5 * (verticals[first] + verticals[second])
            )
        )

    east_flux = face_flux(0, 1)
    west_flux = face_flux(2, 0)
    north_flux = face_flux(0, 3)
    south_flux = face_flux(4, 0)
    return values[0] + wet_sides[0] * (east_flux - west_flux + north_flux - south_flux)


def advance(state, sides):
    state_sides = sides(state, sign_column(STATE_SIGNS), 0)
    tracer = tuple((side[:2] for side in state_sides))
    zonal = tuple((side[2] for side in state_sides))
    meridional = tuple((side[3] for side in state_sides))
    wet_sides = tuple((side[4] for side in state_sides))
    upwind, anti, inflow, outflow = low_order(tracer, zonal, meridional, wet_sides)
    upwind_sides = sides(upwind, sign_column((1.0, 1.0)), 1)
    ratio = ratios(upwind_sides, wet_sides, inflow, outflow)
    ratio_sides = sides(ratio, sign_column((1.0, 1.0, 1.0, 1.0)), 2)
    advected = limited(ratio_sides, upwind, anti, wet_sides[0])
    advected_sides = sides(advected, sign_column((1.0, 1.0)), 3)
    return isopycnal(advected_sides, wet_sides)


def local(
    heat_content_field,
    saltiness_field,
    eastward_cfl_number,
    northward_cfl_number,
    seawater_indicator,
    submerged_layer_total,
    seam_partner_index,
):
    span = heat_content_field.shape[2]
    anchor = lax.axis_index("lon") * span
    on_top = lax.axis_index("lat") == lax.axis_size("lat") - 1
    vertical_layer = jnp.arange(heat_content_field.shape[0], dtype=jnp.int32)[:, None, None]
    submerged_indicator = (
        (seawater_indicator[None] == 1) & (vertical_layer < submerged_layer_total[None])
    ).astype(jnp.float32)
    state = jnp.stack(
        [
            heat_content_field,
            saltiness_field,
            eastward_cfl_number,
            northward_cfl_number,
            submerged_indicator,
        ]
    )
    own_columns = anchor + jnp.arange(span, dtype=jnp.int32)
    facing = jnp.take(seam_partner_index, own_columns)

    def rim_sides(stack, fold_row):
        columns = jnp.concatenate([stack[..., :1], stack[..., -1:]], axis=3)
        column_rim = extended(columns, (("lon", 3),), 1, True)
        rows = jnp.concatenate([stack[:, :, :1, :], stack[:, :, -1:, :]], axis=2)
        row_rim = extended(rows, (("lat", 2),), 1, False)
        north_row = jnp.where(on_top, fold_row, row_rim[:, :, 3:4, :])
        return sided(
            stack, column_rim[..., 0:1], column_rim[..., 3:4], row_rim[:, :, 0:1, :], north_row
        )

    def device_sides(stack, signs, segment):
        top_row = lax.all_gather(stack[:, :, -1:, :], "lon", axis=3, tiled=True)
        fold_row = jnp.take(top_row, facing, axis=3) * signs
        return rim_sides(stack, fold_row)

    final = advance(state, device_sides)
    return (final[0], final[1])


def solution(mesh):
    in_specs = (
        P(None, "lat", "lon"),
        P(None, "lat", "lon"),
        P(None, "lat", "lon"),
        P(None, "lat", "lon"),
        P("lat", "lon"),
        P("lat", "lon"),
        P(),
    )
    out_specs = (P(None, "lat", "lon"), P(None, "lat", "lon"))
    return jax.shard_map(local, mesh=mesh, in_specs=in_specs, out_specs=out_specs, check_vma=False)
```

profile of v0, /device:TPU:97, one launch (start us, length us, event | category | flops | bytes accessed | tf_op | source)
XLA Modules:
  0.0 285.5 jit_solution(14750292049172549492)
XLA Ops:
  4.7 4.7 %collective-permute-start.2 = (f32[5,12,1,128]{3,2,1,0:T(1,128)}, f32[5,12,1,128]{3,2,1,0:T(1,128)}, u32[]{:S(2)}, u32[]{:S(2)}) collective-permute-start(f32[5,12,1,128]{3,2,1,0:T(1,128)} %get-tuple-element.45), channel_id=1, source_target_pairs={{1,0},{2,1},{3,2},{4,3},{5,4},{6,5},{7,6},{9,8},{10,9},{11,10},{12... | collective-permute-start | bytes 92168 | tf_op jit(solution)/shard_map/ppermute | solution.py:26
  9.3 2.7 collective-permute-start.3
  12.0 3.7 %fusion.105 = (f32[5,12,96,1]{3,2,1,0:T(8,128)}, f32[5,12,96,1]{3,2,1,0:T(8,128)}) fusion(f32[5,12,96,128]{3,2,1,0:T(8,128)S(1)} %convert_dynamic-update-slice_fusion), kind=kLoop, calls=%fused_computation.255 | loop fusion | bytes 92160 | tf_op jit(solution)/shard_map/slice | solution.py:222
  15.7 2.9 %copy.952 = f32[5,12,96,1]{2,3,1,0:T(1,128)} copy(f32[5,12,96,1]{3,2,1,0:T(8,128)} %get-tuple-element.41) | data formatting | bytes 46080 | tf_op jit(solution)/shard_map/slice | solution.py:222
  19.9 2.9 %copy.953 = f32[5,12,96,1]{2,3,1,0:T(1,128)} copy(f32[5,12,96,1]{3,2,1,0:T(8,128)} %get-tuple-element.42) | data formatting | bytes 46080 | tf_op jit(solution)/shard_map/slice | solution.py:222
  23.9 22.0 %all_gather.12 = f32[5,12,1,2048]{3,2,1,0:T(1,128)} all-gather(f32[5,12,1,128]{3,2,1,0:T(1,128)} %get-tuple-element.46), channel_id=1, replica_groups=mesh['lon'=16,'lat'=8] {'lon'}, dimensions={3}, use_global_device_ids=true | all-gather | bytes 522240 | tf_op jit(solution)/shard_map/all_gather | solution.py:232
  47.8 3.0 %fusion.106 = (f32[5,12,95,128]{3,2,1,0:T(8,128)}, f32[5,12,95,128]{3,2,1,0:T(8,128)}) fusion(f32[5,12,96,128]{3,2,1,0:T(8,128)S(1)} %convert_dynamic-update-slice_fusion), kind=kLoop, calls=%fused_computation.256 | loop fusion | bytes 11673600 | tf_op jit(solution)/shard_map/jit(_roll_static)/slice | solution.py:44
  50.8 3.6 %fusion.104 = (f32[5,12,96,127]{3,2,1,0:T(8,128)}, f32[5,12,96,127]{3,2,1,0:T(8,128)}) fusion(f32[5,12,96,128]{3,2,1,0:T(8,128)S(1)} %convert_dynamic-update-slice_fusion), kind=kLoop, calls=%fused_computation.254 | loop fusion | bytes 11704320 | tf_op jit(solution)/shard_map/jit(_roll_static)/slice | solution.py:42
  56.6 6.0 %copy.954 = f32[5,12,1,2048]{1,0,3,2:T(8,128)} copy(f32[5,12,1,2048]{3,2,1,0:T(1,128)} %all_gather.12) | data formatting | bytes 983040 | tf_op jit(solution)/shard_map/all_gather | solution.py:232
  62.6 4.9 %gather_fusion.1 = f32[128,5,12]{2,1,0:T(8,128)} fusion(f32[5,12,2048]{1,0,2:T(8,128)} %bitcast.128, s32[1024]{0:T(1024)} %pad_clamp_fusion.1), kind=kCustom, calls=%fused_computation.3 | custom fusion | bytes 61952 | tf_op jit(solution)/shard_map/jit(_take)/gather | solution.py:233
  70.2 3.2 %maximum_select_fusion = f32[5,12,96,128]{3,2,1,0:T(8,128)S(1)} fusion(f32[5,12,96,1]{3,2,1,0:T(8,128)S(1)} %copy-done.5, f32[5,12,96,127]{3,2,1,0:T(8,128)} %get-tuple-element.39, f32[5,12,96]{2,1,0:T(8,128)S(1)} %bitcast.143, pred[128]{0:T(512)(128)(4,1)S(1)} %get-tuple-element.98), kind=kLoop, calls=%fused_computation.19 | loop fusion | flops 1474560 | bytes 5921408 | tf_op jit(solution)/shard_map/jit(_where)/select_n | solution.py:42
  83.3 2.4 copy.1012
  103.3 5.8 %collective-permute-start.6 = (f32[2,12,1,128]{3,2,1,0:T(1,128)}, f32[2,12,1,128]{3,2,1,0:T(1,128)}, u32[]{:S(2)}, u32[]{:S(2)}) collective-permute-start(f32[2,12,1,128]{3,2,1,0:T(1,128)} %get-tuple-element.73), channel_id=1, source_target_pairs={{1,0},{2,1},{3,2},{4,3},{5,4},{6,5},{7,6},{9,8},{10,9},{11,10},{12... | collective-permute-start | bytes 36872 | tf_op jit(solution)/shard_map/ppermute | solution.py:26
  112.8 17.1 %all_gather.13 = f32[2,12,1,2048]{3,0,2,1:T(2,128)S(1)} all-gather(f32[2,12,1,128]{3,0,2,1:T(2,128)} %copy.960), channel_id=1, replica_groups=mesh['lon'=16,'lat'=8] {'lon'}, dimensions={3}, use_global_device_ids=true | all-gather | bytes 208896 | tf_op jit(solution)/shard_map/all_gather | solution.py:232
  129.9 2.3 copy.961
  132.3 2.5 gather_fusion.3
  137.2 10.3 %fusion.12 = (f32[2,12,96,128]{3,2,1,0:T(8,128)S(1)}, f32[2,12,96,128]{3,2,1,0:T(8,128)S(1)}, f32[2,12,96,128]{3,2,1,0:T(8,128)S(1)}, f32[2,12,96,128]{3,2,1,0:T(8,128)S(1)}, f32[2,12,96,128]{3,2,1,0:T(8,128)S(1)}) fusion(f32[2,12,96,128]{3,2,1,0:T(8,128)S(1)} %multiply_subtract_fusion.4, f32[2,12,1,128]{3,2,1,0:T(1,128)} %get-tuple-element.73, ...), kind=kLoop, calls=%fused_computation.41 | loop fusion | flops 17694720 | bytes 27765184 | tf_op jit(solution)/shard_map/min | solution.py:105
  147.6 4.2 %fusion.18 = f32[2,12,96,128]{3,2,1,0:T(8,128)S(1)} fusion(f32[2,12,96,128]{3,2,1,0:T(8,128)S(1)} %multiply_subtract_fusion.4, f32[2,12,1,128]{3,2,1,0:T(1,128)} %get-tuple-element.73, f32[2,12,95,128]{3,2,1,0:T(8,128)S(1)} %copy-done.35, f32[2,12,1,128]{3,2,1,0:T(1,128)} %get-tuple-element.72, f32[2,12,96,128]{3,2,1,0:T(8,128)S(1)} %get-tuple-element.22, ...), kind=kLoop, calls=%fused_computation.47 | loop fusion | flops 7962624 | bytes 12429760 | tf_op jit(solution)/shard_map/min | solution.py:106
  151.8 3.0 %fusion.1 = (f32[4,12,96,1]{3,2,1,0:T(8,128)}, f32[4,12,96,1]{3,2,1,0:T(8,128)}) fusion(f32[2,12,96,128]{3,2,1,0:T(8,128)S(1)} %get-tuple-element.18, f32[2,12,96,128]{3,2,1,0:T(8,128)S(1)} %fusion.18), kind=kLoop, calls=%fused_computation.24 | loop fusion | flops 9216 | bytes 2396160 | tf_op jit(solution)/shard_map/concatenate | solution.py:107
  154.8 3.0 %fusion.2 = (f32[4,12,96,127]{3,2,1,0:T(8,128)}, f32[4,12,96,127]{3,2,1,0:T(8,128)}) fusion(f32[2,12,96,128]{3,2,1,0:T(8,128)S(1)} %get-tuple-element.18, f32[2,12,96,128]{3,2,1,0:T(8,128)S(1)} %fusion.18), kind=kLoop, calls=%fused_computation.25 | loop fusion | flops 1170432 | bytes 7041024 | tf_op jit(solution)/shard_map/concatenate | solution.py:107
  163.4 3.0 %copy.968 = f32[4,12,96,1]{2,0,3,1:T(4,128)} copy(f32[4,12,96,1]{3,2,1,0:T(8,128)} %get-tuple-element.49) | data formatting | bytes 36864 | tf_op jit(solution)/shard_map/slice | solution.py:222
  166.6 3.0 %copy.970 = f32[4,12,96,1]{2,0,3,1:T(4,128)} copy(f32[4,12,96,1]{3,2,1,0:T(8,128)} %get-tuple-element.50) | data formatting | bytes 36864 | tf_op jit(solution)/shard_map/slice | solution.py:222
  171.1 19.1 %all_gather.14 = f32[4,12,1,2048]{3,0,2,1:T(4,128)} all-gather(f32[4,12,1,128]{3,0,2,1:T(4,128)} %copy.972), channel_id=1, replica_groups=mesh['lon'=16,'lat'=8] {'lon'}, dimensions={3}, use_global_device_ids=true | all-gather | bytes 417792 | tf_op jit(solution)/shard_map/all_gather | solution.py:232
  190.3 4.6 %copy.973 = f32[4,12,1,2048]{1,0,3,2:T(4,128)} copy(f32[4,12,1,2048]{3,0,2,1:T(4,128)} %all_gather.14) | data formatting | bytes 786432 | tf_op jit(solution)/shard_map/all_gather | solution.py:232
  194.8 3.8 %gather_fusion.2 = f32[128,4,12]{2,1,0:T(4,128)} fusion(f32[4,12,2048]{1,0,2:T(4,128)} %bitcast.133, s32[1024]{0:T(1024)} %pad_clamp_fusion.1), kind=kCustom, calls=%fused_computation.4 | custom fusion | bytes 49664 | tf_op jit(solution)/shard_map/jit(_take)/gather | solution.py:233
  200.3 6.1 %collective-permute-start.10 = (f32[4,12,1,128]{3,2,1,0:T(1,128)}, f32[4,12,1,128]{3,2,1,0:T(1,128)S(1)}, u32[]{:S(2)}, u32[]{:S(2)}) collective-permute-start(f32[4,12,1,128]{3,2,1,0:T(1,128)} %get-tuple-element.51), channel_id=1, source_target_pairs={{1,0},{2,1},{3,2},{4,3},{5,4},{6,5},{7,6},{9,8},{10,9},{11,10},{12... | collective-permute-start | bytes 73736 | tf_op jit(solution)/shard_map/ppermute | solution.py:26
  207.9 3.2 %maximum_select_fusion.4 = f32[4,12,96,128]{3,2,1,0:T(8,128)S(1)} fusion(f32[4,12,96,1]{3,2,1,0:T(8,128)} %get-tuple-element.49, f32[4,12,96,127]{3,2,1,0:T(8,128)} %get-tuple-element.47, f32[4,12,96]{2,1,0:T(8,128)S(1)} %copy.969, pred[128]{0:T(512)(128)(4,1)S(1)} %get-tuple-element.98), kind=kLoop, calls=%fused_computation.31 | loop fusion | flops 1179648 | bytes 4737152 | tf_op jit(solution)/shard_map/jit(_where)/select_n | solution.py:42
  233.7 18.5 %all_gather.15 = f32[2,12,1,2048]{3,0,2,1:T(2,128)} all-gather(f32[2,12,1,128]{3,0,2,1:T(2,128)} %copy.984), channel_id=1, replica_groups=mesh['lon'=16,'lat'=8] {'lon'}, dimensions={3}, use_global_device_ids=true | all-gather | bytes 208896 | tf_op jit(solution)/shard_map/all_gather | solution.py:232
  252.3 3.7 %copy.985 = f32[2,12,2048]{1,0,2:T(2,128)} copy(f32[2,12,2048]{2,0,1:T(2,128)} %bitcast.135) | data formatting | bytes 393216 | tf_op jit(solution)/shard_map/jit(_take)/Arg_0.21 | solution.py:233
  255.9 3.1 %gather_fusion.4 = f32[128,2,12]{2,1,0:T(2,128)} fusion(f32[2,12,2048]{1,0,2:T(2,128)} %copy.985, s32[1024]{0:T(1024)} %pad_clamp_fusion), kind=kCustom, calls=%fused_computation.1.clone | custom fusion | bytes 25088 | tf_op jit(solution)/shard_map/jit(_take)/gather | solution.py:233
  260.6 5.8 %collective-permute-start.14 = (f32[2,12,1,128]{3,2,1,0:T(1,128)}, f32[2,12,1,128]{3,2,1,0:T(1,128)S(1)}, u32[]{:S(2)}, u32[]{:S(2)}) collective-permute-start(f32[2,12,1,128]{3,2,1,0:T(1,128)} %get-tuple-element.64), channel_id=1, source_target_pairs={{1,0},{2,1},{3,2},{4,3},{5,4},{6,5},{7,6},{9,8},{10,9},{11,10},{12... | collective-permute-start | bytes 36872 | tf_op jit(solution)/shard_map/ppermute | solution.py:26
  280.6 3.8 %multiply_add_fusion = f32[2,12,96,128]{3,2,1,0:T(8,128)S(1)} fusion(f32[2,12,96,128]{3,2,1,0:T(8,128)S(1)} %fusion.23, f32[2,11,96,128]{3,2,1,0:T(8,128)S(1)} %fusion.35, f32[2,11,96,128]{3,2,1,0:T(8,128)S(1)} %fusion.36, f32[2,11,96,128]{3,2,1,0:T(8,128)S(1)} %fusion.37, f32[2,11,96,128]{3,2,1,0:T(8,128)S(1)} %fusion.38, ...), kind=kLoop, calls=%fused_computation.81 | loop fusion | flops 9732096 | bytes 17836480 | tf_op jit(solution)/shard_map/add | solution.py:175
  (301 shorter events, 95.6 us)
Async XLA Ops:
  0.6 45.4 %copy-start = (s32[2048]{0:T(1024)S(1)}, s32[2048]{0:T(1024)}, u32[]{:S(2)}) copy-start(s32[2048]{0:T(1024)} %param.19) | copy-start | bytes 24580
  4.7 74.9 %collective-permute-start.2 = (f32[5,12,1,128]{3,2,1,0:T(1,128)}, f32[5,12,1,128]{3,2,1,0:T(1,128)}, u32[]{:S(2)}, u32[]{:S(2)}) collective-permute-start(f32[5,12,1,128]{3,2,1,0:T(1,128)} %get-tuple-element.45), channel_id=1, source_target_pairs={{1,0},{2,1},{3,2},{4,3},{5,4},{6,5},{7,6},{9,8},{10,9},{11,10},{12... | collective-permute-start | bytes 92168 | tf_op jit(solution)/shard_map/ppermute | solution.py:26
  9.3 74.0 %collective-permute-start.3 = (f32[5,12,1,128]{3,2,1,0:T(1,128)}, f32[5,12,1,128]{3,2,1,0:T(1,128)}, u32[]{:S(2)}, u32[]{:S(2)}) collective-permute-start(f32[5,12,1,128]{3,2,1,0:T(1,128)} %get-tuple-element.46), channel_id=1, source_target_pairs={{0,1},{1,2},{2,3},{3,4},{4,5},{5,6},{6,7},{8,9},{9,10},{10,11},{11... | collective-permute-start | bytes 92168 | tf_op jit(solution)/shard_map/ppermute | solution.py:24
  18.6 50.8 %collective-permute-start = (f32[5,12,96,1]{2,3,1,0:T(1,128)}, f32[5,12,96,1]{2,3,1,0:T(1,128)}, u32[]{:S(2)}, u32[]{:S(2)}) collective-permute-start(f32[5,12,96,1]{2,3,1,0:T(1,128)} %copy.952), channel_id=1, source_target_pairs={{8,0},{16,8},{24,16},{32,24},{40,32},{48,40},{56,48},{64,56},{72,6... | collective-permute-start | bytes 69128 | tf_op jit(solution)/shard_map/ppermute | solution.py:26
  22.7 52.5 %collective-permute-start.1 = (f32[5,12,96,1]{2,3,1,0:T(1,128)}, f32[5,12,96,1]{2,3,1,0:T(1,128)}, u32[]{:S(2)}, u32[]{:S(2)}) collective-permute-start(f32[5,12,96,1]{2,3,1,0:T(1,128)} %copy.953), channel_id=1, source_target_pairs={{0,8},{8,16},{16,24},{24,32},{32,40},{40,48},{48,56},{56,64},{64,7... | collective-permute-start | bytes 69128 | tf_op jit(solution)/shard_map/ppermute | solution.py:24
  54.5 35.1 %copy-start.11 = (f32[12,96,128]{2,1,0:T(8,128)}, f32[12,96,128]{2,1,0:T(8,128)S(1)}, u32[]{:S(2)}) copy-start(f32[12,96,128]{2,1,0:T(8,128)S(1)} %fusion.83) | copy-start | bytes 1769476
  56.6 211.3 %copy-start.83 = (pred[128]{0:T(512)(128)(4,1)}, pred[128]{0:T(512)(128)(4,1)S(1)}, u32[]{:S(2)}) copy-start(pred[128]{0:T(512)(128)(4,1)S(1)} %get-tuple-element.98) | copy-start | bytes 388
  56.6 213.4 %copy-start.81 = (pred[128]{0:T(512)(128)(4,1)}, pred[128]{0:T(512)(128)(4,1)S(1)}, u32[]{:S(2)}) copy-start(pred[128]{0:T(512)(128)(4,1)S(1)} %get-tuple-element.97) | copy-start | bytes 388
  56.6 13.5 %copy-start.5 = (f32[5,12,96,1]{3,2,1,0:T(8,128)S(1)}, f32[5,12,96,1]{3,2,1,0:T(8,128)}, u32[]{:S(2)}) copy-start(f32[5,12,96,1]{3,2,1,0:T(8,128)} %get-tuple-element.41) | copy-start | bytes 69124
  73.4 16.2 %copy-start.8 = (f32[5,12,96,128]{3,2,1,0:T(8,128)}, f32[5,12,96,128]{3,2,1,0:T(8,128)S(1)}, u32[]{:S(2)}) copy-start(f32[5,12,96,128]{3,2,1,0:T(8,128)S(1)} %maximum_select_fusion) | copy-start | bytes 8847364
  77.7 11.9 %copy-start.9 = (f32[5,12,96,128]{3,2,1,0:T(8,128)}, f32[5,12,96,128]{3,2,1,0:T(8,128)S(1)}, u32[]{:S(2)}) copy-start(f32[5,12,96,128]{3,2,1,0:T(8,128)S(1)} %maximum_select_fusion.1) | copy-start | bytes 8847364
  81.9 19.7 %copy-start.6 = (f32[5,12,96,128]{3,2,1,0:T(8,128)}, f32[5,12,96,128]{3,2,1,0:T(8,128)S(1)}, u32[]{:S(2)}) copy-start(f32[5,12,96,128]{3,2,1,0:T(8,128)S(1)} %maximum_select_fusion.2) | copy-start | bytes 8847364
  87.4 15.1 %copy-start.7 = (f32[5,12,96,128]{3,2,1,0:T(8,128)}, f32[5,12,96,128]{3,2,1,0:T(8,128)S(1)}, u32[]{:S(2)}) copy-start(f32[5,12,96,128]{3,2,1,0:T(8,128)S(1)} %maximum_select_fusion.3) | copy-start | bytes 8847364
  92.8 18.0 %copy-start.15 = (f32[2,12,96,1]{3,2,1,0:T(8,128)}, f32[2,12,96,1]{3,2,1,0:T(8,128)S(1)}, u32[]{:S(2)}) copy-start(f32[2,12,96,1]{3,2,1,0:T(8,128)S(1)} %get-tuple-element.69) | copy-start | bytes 27652
  92.8 44.3 %copy-start.14 = (f32[2,12,96,1]{3,2,1,0:T(8,128)}, f32[2,12,96,1]{3,2,1,0:T(8,128)S(1)}, u32[]{:S(2)}) copy-start(f32[2,12,96,1]{3,2,1,0:T(8,128)S(1)} %get-tuple-element.68) | copy-start | bytes 27652
  98.0 38.3 %collective-permute-start.7 = (f32[2,12,1,128]{3,2,1,0:T(1,128)}, f32[2,12,1,128]{3,2,1,0:T(1,128)}, u32[]{:S(2)}, u32[]{:S(2)}) collective-permute-start(f32[2,12,1,128]{3,2,1,0:T(1,128)} %get-tuple-element.72), channel_id=1, source_target_pairs={{0,1},{1,2},{2,3},{3,4},{4,5},{5,6},{6,7},{8,9},{9,10},{10,11},{11... | collective-permute-start | bytes 36872 | tf_op jit(solution)/shard_map/ppermute | solution.py:24
  103.3 32.2 %collective-permute-start.6 = (f32[2,12,1,128]{3,2,1,0:T(1,128)}, f32[2,12,1,128]{3,2,1,0:T(1,128)}, u32[]{:S(2)}, u32[]{:S(2)}) collective-permute-start(f32[2,12,1,128]{3,2,1,0:T(1,128)} %get-tuple-element.73), channel_id=1, source_target_pairs={{1,0},{2,1},{3,2},{4,3},{5,4},{6,5},{7,6},{9,8},{10,9},{11,10},{12... | collective-permute-start | bytes 36872 | tf_op jit(solution)/shard_map/ppermute | solution.py:26
  110.1 24.7 %collective-permute-start.4 = (f32[2,12,96,1]{2,0,3,1:T(2,128)}, f32[2,12,96,1]{2,0,3,1:T(2,128)}, u32[]{:S(2)}, u32[]{:S(2)}) collective-permute-start(f32[2,12,96,1]{2,0,3,1:T(2,128)} %copy.956), channel_id=1, source_target_pairs={{8,0},{16,8},{24,16},{32,24},{40,32},{48,40},{56,48},{64,56},{72,6... | collective-permute-start | bytes 27656 | tf_op jit(solution)/shard_map/ppermute | solution.py:26
  111.8 23.8 %collective-permute-start.5 = (f32[2,12,96,1]{2,0,3,1:T(2,128)}, f32[2,12,96,1]{2,0,3,1:T(2,128)S(1)}, u32[]{:S(2)}, u32[]{:S(2)}) collective-permute-start(f32[2,12,96,1]{2,0,3,1:T(2,128)} %copy.958), channel_id=1, source_target_pairs={{0,8},{8,16},{16,24},{24,32},{32,40},{40,48},{48,56},{56,64},{64,7... | collective-permute-start | bytes 27656 | tf_op jit(solution)/shard_map/ppermute | solution.py:24
  137.1 10.5 %copy-start.16 = (f32[2,12,96,1]{3,2,1,0:T(8,128)S(1)}, f32[2,12,96,1]{3,2,1,0:T(8,128)}, u32[]{:S(2)}) copy-start(f32[2,12,96,1]{3,2,1,0:T(8,128)} %copy-done.15) | copy-start | bytes 27652
  137.1 10.5 %copy-start.32 = (f32[2,12,96,127]{3,2,1,0:T(8,128)S(1)}, f32[2,12,96,127]{3,2,1,0:T(8,128)}, u32[]{:S(2)}) copy-start(f32[2,12,96,127]{3,2,1,0:T(8,128)} %get-tuple-element.66) | copy-start | bytes 3511300
  137.1 10.5 %copy-start.33 = (f32[2,12,96,127]{3,2,1,0:T(8,128)S(1)}, f32[2,12,96,127]{3,2,1,0:T(8,128)}, u32[]{:S(2)}) copy-start(f32[2,12,96,127]{3,2,1,0:T(8,128)} %get-tuple-element.67) | copy-start | bytes 3511300
  137.1 10.5 %copy-start.34 = (f32[2,12,95,128]{3,2,1,0:T(8,128)S(1)}, f32[2,12,95,128]{3,2,1,0:T(8,128)}, u32[]{:S(2)}) copy-start(f32[2,12,95,128]{3,2,1,0:T(8,128)} %get-tuple-element.70) | copy-start | bytes 3502084
  151.8 62.1 %copy-start.2 = (f32[2,12,96,128]{3,2,1,0:T(8,128)}, f32[2,12,96,128]{3,2,1,0:T(8,128)S(1)}, u32[]{:S(2)}) copy-start(f32[2,12,96,128]{3,2,1,0:T(8,128)S(1)} %fusion.18) | copy-start | bytes 3538948
  161.5 51.7 %collective-permute-start.11 = (f32[4,12,1,128]{3,2,1,0:T(1,128)}, f32[4,12,1,128]{3,2,1,0:T(1,128)}, u32[]{:S(2)}, u32[]{:S(2)}) collective-permute-start(f32[4,12,1,128]{3,2,1,0:T(1,128)} %get-tuple-element.52), channel_id=1, source_target_pairs={{0,1},{1,2},{2,3},{3,4},{4,5},{5,6},{6,7},{8,9},{9,10},{10,11},{11... | collective-permute-start | bytes 73736 | tf_op jit(solution)/shard_map/ppermute | solution.py:24
  166.4 40.0 %collective-permute-start.8 = (f32[4,12,96,1]{2,0,3,1:T(4,128)}, f32[4,12,96,1]{2,0,3,1:T(4,128)}, u32[]{:S(2)}, u32[]{:S(2)}) collective-permute-start(f32[4,12,96,1]{2,0,3,1:T(4,128)} %copy.968), channel_id=1, source_target_pairs={{8,0},{16,8},{24,16},{32,24},{40,32},{48,40},{56,48},{64,56},{72,6... | collective-permute-start | bytes 55304 | tf_op jit(solution)/shard_map/ppermute | solution.py:26
  169.6 37.6 %collective-permute-start.9 = (f32[4,12,96,1]{2,0,3,1:T(4,128)}, f32[4,12,96,1]{2,0,3,1:T(4,128)}, u32[]{:S(2)}, u32[]{:S(2)}) collective-permute-start(f32[4,12,96,1]{2,0,3,1:T(4,128)} %copy.970), channel_id=1, source_target_pairs={{0,8},{8,16},{16,24},{24,32},{32,40},{40,48},{48,56},{56,64},{64,7... | collective-permute-start | bytes 55304 | tf_op jit(solution)/shard_map/ppermute | solution.py:24
  200.3 12.8 %collective-permute-start.10 = (f32[4,12,1,128]{3,2,1,0:T(1,128)}, f32[4,12,1,128]{3,2,1,0:T(1,128)S(1)}, u32[]{:S(2)}, u32[]{:S(2)}) collective-permute-start(f32[4,12,1,128]{3,2,1,0:T(1,128)} %get-tuple-element.51), channel_id=1, source_target_pairs={{1,0},{2,1},{3,2},{4,3},{5,4},{6,5},{7,6},{9,8},{10,9},{11,10},{12... | collective-permute-start | bytes 73736 | tf_op jit(solution)/shard_map/ppermute | solution.py:26
  225.9 48.3 %collective-permute-start.15 = (f32[2,12,1,128]{3,2,1,0:T(1,128)}, f32[2,12,1,128]{3,2,1,0:T(1,128)}, u32[]{:S(2)}, u32[]{:S(2)}) collective-permute-start(f32[2,12,1,128]{3,2,1,0:T(1,128)} %get-tuple-element.65), channel_id=1, source_target_pairs={{0,1},{1,2},{2,3},{3,4},{4,5},{5,6},{6,7},{8,9},{9,10},{10,11},{11... | collective-permute-start | bytes 36872 | tf_op jit(solution)/shard_map/ppermute | solution.py:24
  228.8 37.6 %collective-permute-start.12 = (f32[2,12,96,1]{2,0,3,1:T(2,128)}, f32[2,12,96,1]{2,0,3,1:T(2,128)}, u32[]{:S(2)}, u32[]{:S(2)}) collective-permute-start(f32[2,12,96,1]{2,0,3,1:T(2,128)} %copy.980), channel_id=1, source_target_pairs={{8,0},{16,8},{24,16},{32,24},{40,32},{48,40},{56,48},{64,56},{72,6... | collective-permute-start | bytes 27656 | tf_op jit(solution)/shard_map/ppermute | solution.py:26
  232.4 34.7 %collective-permute-start.13 = (f32[2,12,96,1]{2,0,3,1:T(2,128)}, f32[2,12,96,1]{2,0,3,1:T(2,128)}, u32[]{:S(2)}, u32[]{:S(2)}) collective-permute-start(f32[2,12,96,1]{2,0,3,1:T(2,128)} %copy.982), channel_id=1, source_target_pairs={{0,8},{8,16},{16,24},{24,32},{32,40},{40,48},{48,56},{56,64},{64,7... | collective-permute-start | bytes 27656 | tf_op jit(solution)/shard_map/ppermute | solution.py:24
  260.6 13.4 %collective-permute-start.14 = (f32[2,12,1,128]{3,2,1,0:T(1,128)}, f32[2,12,1,128]{3,2,1,0:T(1,128)S(1)}, u32[]{:S(2)}, u32[]{:S(2)}) collective-permute-start(f32[2,12,1,128]{3,2,1,0:T(1,128)} %get-tuple-element.64), channel_id=1, source_target_pairs={{1,0},{2,1},{3,2},{4,3},{5,4},{6,5},{7,6},{9,8},{10,9},{11,10},{12... | collective-permute-start | bytes 36872 | tf_op jit(solution)/shard_map/ppermute | solution.py:26
  (74 other events, 223.3 us)
where the time goes:
time: 288 us; the launch traced here: 286 us
  local copies, waits for them, and re-layouts  99.8 us (35%)
  blocking collectives  76.8 us (27%)
  other arithmetic  68.2 us (24%)
  starting transfers between devices  38.6 us (13%)
    all_gather x4, blocking collectives, device_sides(): top_row = lax.all_gather(stack[:, :, -1:, :], 'lon', axis=3, tiled=True)  76.8 us
    ppermute x8, starting transfers between devices, extended(): lax.ppermute(head, axis, [((i + 1) % count, i) for i in range(ends)])  24.9 us
    slice x11, local copies, waits for them, and re-layouts, rim_sides(): columns = jnp.concatenate([stack[..., :1], stack[..., -1:]], axis=3)  20.1 us
    gather x8, local copies, waits for them, and re-layouts, device_sides(): fold_row = jnp.take(top_row, facing, axis=3) * signs  19.4 us
    unnamed x188, local copies, waits for them, and re-layouts  15.6 us
    ppermute x8, starting transfers between devices, extended(): lax.ppermute(tail, axis, [(i, (i + 1) % count) for i in range(ends)])  13.7 us
    all_gather x3, local copies, waits for them, and re-layouts, device_sides(): top_row = lax.all_gather(stack[:, :, -1:, :], 'lon', axis=3, tiled=True)  12.9 us
    min x1, other arithmetic, ratios(): jnp.minimum(1.0, (highest - value_centre) / jnp.maximum(inflow, RATIO_FLO...  10.3 us
  transfers between devices with their start and end apart: 16, of which 0 were waited for; matrix products, arithmetic and copies ran while one was open for 34% of the time, Pallas kernels for 0%

commit v1 on v0

--- a/solution.py
+++ b/solution.py
@@ -229,7 +229,10 @@
         )
 
     def device_sides(stack, signs, segment):
-        top_row = lax.all_gather(stack[:, :, -1:, :], "lon", axis=3, tiled=True)
+        top_row = jnp.concatenate(
+            lax.all_to_all(jnp.stack([stack[:, :, -1:, :]] * lax.axis_size("lon")), "lon", 0, 0),
+            axis=3,
+        )
         fold_row = jnp.take(top_row, facing, axis=3) * signs
         return rim_sides(stack, fold_row)
 

time: 288 us -> 269 us (0.934)
  blocking collectives: 76.8 us -> 0 us
  starting transfers between devices: 38.6 us -> 68.5 us
  other arithmetic: 68.2 us -> 90.7 us
  local copies, waits for them, and re-layouts: 99.8 us -> 105 us
    all_gather x4 -> x0, blocking collectives: 76.8 us -> none  [device_sides(): top_row = lax.all_gather(stack[:, :, -1:, :], 'lon', axis=3, tiled=True)]
    all_to_all x0 -> x4, starting transfers between devices: none -> 24.6 us  [device_sides(): lax.all_to_all(jnp.stack([stack[:, :, -1:, :]] * lax.axis_size('lon')), '...]
    unnamed x188 -> x222, local copies, waits for them, and re-layouts: 15.6 us -> 28.9 us
    reshape x0 -> x4, local copies, waits for them, and re-layouts: none -> 12.9 us  [device_sides(): jnp.concatenate(lax.all_to_all(jnp.stack([stack[:, :, -1:, :]] * lax.axis...]
    all_gather x3 -> x0, local copies, waits for them, and re-layouts: 12.9 us -> none  [device_sides(): top_row = lax.all_gather(stack[:, :, -1:, :], 'lon', axis=3, tiled=True)]
    slice x11 -> x7, local copies, waits for them, and re-layouts: 20.1 us -> 8.37 us  [rim_sides(): columns = jnp.concatenate([stack[..., :1], stack[..., -1:]], axis=3)]
    select_n x3, other arithmetic: 1.97 us -> 6.33 us  [sided(): jnp.where(level == height - 1, north_row, jnp.roll(core, -1, axis=-2))]
    gather x8 -> x7, local copies, waits for them, and re-layouts: 19.4 us -> 15.4 us  [device_sides(): fold_row = jnp.take(top_row, facing, axis=3) * signs]
  transfers between devices with their start and end apart: 16 -> 20, of which waited for: 0 -> 0; matrix products, arithmetic and copies ran while one was open for 34% -> 43% of each run, Pallas kernels for 0% -> 0%
where the time goes in v1:
time: 269 us; the launch traced here: 266 us
  local copies, waits for them, and re-layouts  105 us (39%)
  other arithmetic  90.7 us (34%)
  starting transfers between devices  68.5 us (25%)
    unnamed x222, local copies, waits for them, and re-layouts  28.9 us
    ppermute x8, starting transfers between devices, extended(): lax.ppermute(head, axis, [((i + 1) % count, i) for i in range(ends)])  26.2 us
    all_to_all x4, starting transfers between devices, device_sides(): lax.all_to_all(jnp.stack([stack[:, :, -1:, :]] * lax.axis_size('lon')), '...  24.6 us
    ppermute x8, starting transfers between devices, extended(): lax.ppermute(tail, axis, [(i, (i + 1) % count) for i in range(ends)])  17.7 us
    gather x7, local copies, waits for them, and re-layouts, device_sides(): fold_row = jnp.take(top_row, facing, axis=3) * signs  15.4 us
    reshape x4, local copies, waits for them, and re-layouts, device_sides(): jnp.concatenate(lax.all_to_all(jnp.stack([stack[:, :, -1:, :]] * lax.axis...  12.9 us
    min x1, other arithmetic, ratios(): jnp.minimum(1.0, (highest - value_centre) / jnp.maximum(inflow, RATIO_FLO...  10.3 us
    select_n x3, other arithmetic, sided(): jnp.where(lane == width - 1, east_col, jnp.roll(core, -1, axis=-1))  9.95 us
  transfers between devices with their start and end apart: 20, of which 0 were waited for; matrix products, arithmetic and copies ran while one was open for 43% of the time, Pallas kernels for 0%

profile of v1, /device:TPU:97, one launch (start us, length us, event | category | flops | bytes accessed | tf_op | source)
XLA Modules:
  0.0 266.1 jit_solution(12086486455971761519)
XLA Ops:
  4.6 4.8 %collective-permute-start.3 = (f32[5,12,1,128]{3,2,1,0:T(1,128)}, f32[5,12,1,128]{3,2,1,0:T(1,128)}, u32[]{:S(2)}, u32[]{:S(2)}) collective-permute-start(f32[5,12,1,128]{3,2,1,0:T(1,128)} %get-tuple-element.38), channel_id=1, source_target_pairs={{0,1},{1,2},{2,3},{3,4},{4,5},{5,6},{6,7},{8,9},{9,10},{10,11},{11... | collective-permute-start | bytes 92168 | tf_op jit(solution)/shard_map/ppermute | solution.py:24
  11.3 5.4 %all-to-all-start = ((f32[16,5,12,1,128]{4,3,2,1,0:T(1,128)}), f32[16,5,12,1,128]{4,3,2,1,0:T(1,128)}, u32[]{:S(2)}, u32[]{:S(2)}) async-start(f32[16,5,12,1,128]{4,3,2,1,0:T(1,128)} %stack.26), calls=%async_computation | async-start | bytes 983040 | tf_op jit(solution)/shard_map/all_to_all | solution.py:233
  17.6 4.4 %collective-permute-start.2 = (f32[5,12,1,128]{1,0,3,2:T(8,128)}, f32[5,12,1,128]{1,0,3,2:T(8,128)}, u32[]{:S(2)}, u32[]{:S(2)}) collective-permute-start(f32[5,12,1,128]{1,0,3,2:T(8,128)} %copy.309), channel_id=1, source_target_pairs={{1,0},{2,1},{3,2},{4,3},{5,4},{6,5},{7,6},{9,8},{10,9},{11,10},{12... | collective-permute-start | bytes 92168 | tf_op jit(solution)/shard_map/ppermute | solution.py:26
  22.0 3.7 %fusion.109 = (f32[5,12,96,1]{3,2,1,0:T(8,128)}, f32[5,12,96,1]{3,2,1,0:T(8,128)}) fusion(f32[5,12,96,128]{3,2,1,0:T(8,128)S(1)} %convert_dynamic-update-slice_fusion), kind=kLoop, calls=%fused_computation.257 | loop fusion | bytes 92160 | tf_op jit(solution)/shard_map/slice | solution.py:222
  25.7 3.6 %copy.307 = f32[5,12,96,1]{2,1,0,3:T(8,128)} copy(f32[5,12,96,1]{3,2,1,0:T(8,128)} %get-tuple-element.33) | data formatting | bytes 46080
  29.7 3.6 %copy.308 = f32[5,12,96,1]{2,1,0,3:T(8,128)} copy(f32[5,12,96,1]{3,2,1,0:T(8,128)} %get-tuple-element.34) | data formatting | bytes 46080
  36.5 3.1 %fusion.110 = (f32[5,12,95,128]{3,2,1,0:T(8,128)}, f32[5,12,95,128]{3,2,1,0:T(8,128)}) fusion(f32[5,12,96,128]{3,2,1,0:T(8,128)S(1)} %convert_dynamic-update-slice_fusion), kind=kLoop, calls=%fused_computation.258 | loop fusion | bytes 11673600 | tf_op jit(solution)/shard_map/jit(_roll_static)/slice | solution.py:44
  39.6 3.8 %fusion.108 = (f32[5,12,96,127]{3,2,1,0:T(8,128)}, f32[5,12,96,127]{3,2,1,0:T(8,128)}) fusion(f32[5,12,96,128]{3,2,1,0:T(8,128)S(1)} %convert_dynamic-update-slice_fusion), kind=kLoop, calls=%fused_computation.256 | loop fusion | bytes 11704320 | tf_op jit(solution)/shard_map/jit(_roll_static)/slice | solution.py:42
  45.5 3.7 %maximum_select_fusion = f32[5,12,96,128]{3,2,1,0:T(8,128)S(1)} fusion(f32[5,12,96,1]{3,2,1,0:T(8,128)} %get-tuple-element.33, f32[5,12,96,127]{3,2,1,0:T(8,128)} %get-tuple-element.31, f32[5,12,96]{2,1,0:T(8,128)} %bitcast.4, pred[128]{0:T(512)(128)(4,1)S(1)} %get-tuple-element.90), kind=kLoop, calls=%fused_computation.19 | loop fusion | flops 1474560 | bytes 5921408 | tf_op jit(solution)/shard_map/jit(_where)/select_n | solution.py:42
  59.7 5.8 %copy.295 = f32[5,12,1,16,128]{1,0,4,3,2:T(8,128)} copy(f32[5,12,1,16,128]{4,2,1,0,3:T(1,128)} %bitcast.11) | data formatting | bytes 983040 | tf_op jit(solution)/shard_map/reshape | solution.py:232
  65.6 4.9 %gather_fusion.1 = f32[128,5,12]{2,1,0:T(8,128)} fusion(f32[5,12,2048]{1,0,2:T(8,128)} %bitcast.155, s32[1024]{0:T(1024)} %pad_clamp_fusion.1), kind=kCustom, calls=%fused_computation.3 | custom fusion | bytes 61952 | tf_op jit(solution)/shard_map/jit(_take)/gather | solution.py:236
  91.4 3.8 %collective-permute-start.7 = (f32[2,12,1,128]{3,2,1,0:T(1,128)}, f32[2,12,1,128]{3,2,1,0:T(1,128)}, u32[]{:S(2)}, u32[]{:S(2)}) collective-permute-start(f32[2,12,1,128]{3,2,1,0:T(1,128)} %get-tuple-element.64), channel_id=1, source_target_pairs={{0,1},{1,2},{2,3},{3,4},{4,5},{5,6},{6,7},{8,9},{9,10},{10,11},{11... | collective-permute-start | bytes 36872 | tf_op jit(solution)/shard_map/ppermute | solution.py:24
  96.9 6.5 %all-to-all-start.1 = ((f32[16,2,12,1,128]{4,3,2,1,0:T(1,128)}), f32[16,2,12,1,128]{4,3,2,1,0:T(1,128)}, u32[]{:S(2)}, u32[]{:S(2)}) async-start(f32[16,2,12,1,128]{4,3,2,1,0:T(1,128)} %stack.27), calls=%async_computation.1 | async-start | bytes 393216 | tf_op jit(solution)/shard_map/all_to_all | solution.py:233
  103.4 4.6 %collective-permute-start.6 = (f32[2,12,1,128]{3,2,1,0:T(1,128)}, f32[2,12,1,128]{3,2,1,0:T(1,128)}, u32[]{:S(2)}, u32[]{:S(2)}) collective-permute-start(f32[2,12,1,128]{3,2,1,0:T(1,128)} %get-tuple-element.65), channel_id=1, source_target_pairs={{1,0},{2,1},{3,2},{4,3},{5,4},{6,5},{7,6},{9,8},{10,9},{11,10},{12... | collective-permute-start | bytes 36872 | tf_op jit(solution)/shard_map/ppermute | solution.py:26
  123.6 10.3 %fusion.12 = (f32[2,12,96,128]{3,2,1,0:T(8,128)S(1)}, f32[2,12,96,128]{3,2,1,0:T(8,128)S(1)}, f32[2,12,96,128]{3,2,1,0:T(8,128)S(1)}, f32[2,12,96,128]{3,2,1,0:T(8,128)S(1)}, f32[2,12,96,128]{3,2,1,0:T(8,128)S(1)}) fusion(f32[2,12,96,128]{3,2,1,0:T(8,128)S(1)} %multiply_subtract_fusion.4, f32[2,12,1,128]{3,2,1,0:T(1,128)} %get-tuple-element.65, ...), kind=kLoop, calls=%fused_computation.41 | loop fusion | flops 17694720 | bytes 27765184 | tf_op jit(solution)/shard_map/min | solution.py:105
  134.1 4.1 %fusion.18 = f32[2,12,96,128]{3,2,1,0:T(8,128)S(1)} fusion(f32[2,12,96,128]{3,2,1,0:T(8,128)S(1)} %multiply_subtract_fusion.4, f32[2,12,1,128]{3,2,1,0:T(1,128)S(1)} %copy-done.96, f32[2,12,95,128]{3,2,1,0:T(8,128)S(1)} %copy-done.39, f32[2,12,1,128]{3,2,1,0:T(1,128)} %get-tuple-element.64, f32[2,12,96,128]{3,2,1,0:T(8,128)S(1)} %get-tuple-element.14, ...), kind=kLoop, calls=%fused_computation.47 | loop fusion | flops 7962624 | bytes 12429760 | tf_op jit(solution)/shard_map/min | solution.py:106
  138.2 3.0 %fusion.1 = (f32[4,12,96,1]{3,2,1,0:T(8,128)}, f32[4,12,96,1]{3,2,1,0:T(8,128)}) fusion(f32[2,12,96,128]{3,2,1,0:T(8,128)S(1)} %get-tuple-element.10, f32[2,12,96,128]{3,2,1,0:T(8,128)S(1)} %fusion.18), kind=kLoop, calls=%fused_computation.24 | loop fusion | flops 9216 | bytes 2396160 | tf_op jit(solution)/shard_map/concatenate | solution.py:107
  141.2 3.2 %fusion.2 = (f32[4,12,96,127]{3,2,1,0:T(8,128)}, f32[4,12,96,127]{3,2,1,0:T(8,128)}) fusion(f32[2,12,96,128]{3,2,1,0:T(8,128)S(1)} %get-tuple-element.10, f32[2,12,96,128]{3,2,1,0:T(8,128)S(1)} %fusion.18), kind=kLoop, calls=%fused_computation.25 | loop fusion | flops 1170432 | bytes 7041024 | tf_op jit(solution)/shard_map/concatenate | solution.py:107
  146.0 3.0 %copy.310 = f32[4,12,96,1]{2,0,3,1:T(4,128)} copy(f32[4,12,96,1]{3,2,1,0:T(8,128)} %get-tuple-element.41) | data formatting | bytes 36864
  149.0 3.9 %collective-permute-start.8 = (f32[4,12,96,1]{2,0,3,1:T(4,128)}, f32[4,12,96,1]{2,0,3,1:T(4,128)}, u32[]{:S(2)}, u32[]{:S(2)}) collective-permute-start(f32[4,12,96,1]{2,0,3,1:T(4,128)} %copy.310), channel_id=1, source_target_pairs={{8,0},{16,8},{24,16},{32,24},{40,32},{48,40},{56,48},{64,56},{72,6... | collective-permute-start | bytes 55304 | tf_op jit(solution)/shard_map/ppermute | solution.py:26
  157.3 3.2 %collective-permute-start.11 = (f32[4,12,1,128]{3,2,1,0:T(1,128)}, f32[4,12,1,128]{3,2,1,0:T(1,128)}, u32[]{:S(2)}, u32[]{:S(2)}) collective-permute-start(f32[4,12,1,128]{3,2,1,0:T(1,128)} %get-tuple-element.44), channel_id=1, source_target_pairs={{0,1},{1,2},{2,3},{3,4},{4,5},{5,6},{6,7},{8,9},{9,10},{10,11},{11... | collective-permute-start | bytes 73736 | tf_op jit(solution)/shard_map/ppermute | solution.py:24
  161.3 6.1 %all-to-all-start.2 = ((f32[16,4,12,1,128]{4,1,2,3,0:T(4,128)}), f32[16,4,12,1,128]{4,1,2,3,0:T(4,128)}, u32[]{:S(2)}, u32[]{:S(2)}) async-start(f32[16,4,12,1,128]{4,1,2,3,0:T(4,128)} %stack.28), calls=%async_computation.2 | async-start | bytes 786432 | tf_op jit(solution)/shard_map/all_to_all | solution.py:233
  168.7 5.7 %collective-permute-start.10 = (f32[4,12,1,128]{3,0,1,2:T(4,128)}, f32[4,12,1,128]{3,0,1,2:T(4,128)}, u32[]{:S(2)}, u32[]{:S(2)}) collective-permute-start(f32[4,12,1,128]{3,0,1,2:T(4,128)} %copy.312), channel_id=1, source_target_pairs={{1,0},{2,1},{3,2},{4,3},{5,4},{6,5},{7,6},{9,8},{10,9},{11,10},{12... | collective-permute-start | bytes 73736 | tf_op jit(solution)/shard_map/ppermute | solution.py:26
  175.8 4.2 %maximum_select_fusion.4 = f32[4,12,96,128]{3,2,1,0:T(8,128)} fusion(f32[4,12,96,1]{3,2,1,0:T(8,128)} %get-tuple-element.41, f32[4,12,96,127]{3,2,1,0:T(8,128)} %get-tuple-element.39, f32[4,12,96]{2,1,0:T(8,128)S(1)} %copy.266, pred[128]{0:T(512)(128)(4,1)S(1)} %get-tuple-element.90), kind=kLoop, calls=%fused_computation.31 | loop fusion | flops 1179648 | bytes 4737152 | tf_op jit(solution)/shard_map/jit(_where)/select_n | solution.py:42
  186.1 4.5 %copy.299 = f32[4,12,1,16,128]{1,0,4,3,2:T(4,128)} copy(f32[4,12,1,16,128]{4,0,1,2,3:T(4,128)} %bitcast.42) | data formatting | bytes 786432 | tf_op jit(solution)/shard_map/reshape | solution.py:232
  190.6 3.1 %gather_fusion.2 = f32[128,4,12]{2,1,0:T(4,128)S(1)} fusion(f32[4,12,2048]{1,0,2:T(4,128)} %bitcast.160, s32[1024]{0:T(1024)} %pad_clamp_fusion.1), kind=kCustom, calls=%fused_computation.4 | custom fusion | bytes 49664 | tf_op jit(solution)/shard_map/jit(_take)/gather | solution.py:236
  197.5 4.5 %fusion.23 = f32[2,12,96,128]{3,2,1,0:T(8,128)S(1)} fusion(f32[2,12,96,128]{3,2,1,0:T(8,128)S(1)} %multiply_subtract_fusion.4, f32[2,12,96,128]{3,2,1,0:T(8,128)} %copy-done.29, f32[2,12,96,128]{3,2,1,0:T(8,128)S(1)} %copy-done.3, f32[4,12,96,128]{3,2,1,0:T(8,128)} %fusion.6, f32[2,12,96,128]{3,2,1,0:T(8,128)S(1)} %get-tuple-element.10, ...), kind=kLoop, calls=%fused_computation.53 | loop fusion | flops 7372800 | bytes 19464192 | tf_op jit(solution)/shard_map/sub | solution.py:132
  215.8 6.7 %all-to-all-start.3 = ((f32[16,2,12,1,128]{4,3,2,1,0:T(1,128)}), f32[16,2,12,1,128]{4,3,2,1,0:T(1,128)}, u32[]{:S(2)}, u32[]{:S(2)}) async-start(f32[16,2,12,1,128]{4,3,2,1,0:T(1,128)} %stack.29), calls=%async_computation.3 | async-start | bytes 393216 | tf_op jit(solution)/shard_map/all_to_all | solution.py:233
  222.4 6.4 %collective-permute-start.14 = (f32[2,12,1,128]{3,2,1,0:T(1,128)}, f32[2,12,1,128]{3,2,1,0:T(1,128)}, u32[]{:S(2)}, u32[]{:S(2)}) collective-permute-start(f32[2,12,1,128]{3,2,1,0:T(1,128)} %get-tuple-element.56), channel_id=1, source_target_pairs={{1,0},{2,1},{3,2},{4,3},{5,4},{6,5},{7,6},{9,8},{10,9},{11,10},{12... | collective-permute-start | bytes 36872 | tf_op jit(solution)/shard_map/ppermute | solution.py:26
  244.4 3.6 %copy.300 = f32[2,12,1,2048]{1,0,3,2:T(2,128)} copy(f32[2,12,1,2048]{3,2,1,0:T(1,128)} %bitcast.164) | data formatting | bytes 393216 | tf_op jit(solution)/shard_map/jit(_take)/Arg_0.21 | solution.py:236
  248.0 3.1 %gather_fusion.4 = f32[128,2,12]{2,1,0:T(2,128)} fusion(f32[2,12,2048]{1,0,2:T(2,128)} %bitcast.161, s32[1024]{0:T(1024)} %pad_clamp_fusion), kind=kCustom, calls=%fused_computation.1.clone | custom fusion | bytes 25088 | tf_op jit(solution)/shard_map/jit(_take)/gather | solution.py:236
  261.2 3.8 %multiply_add_fusion = f32[2,12,96,128]{3,2,1,0:T(8,128)S(1)} fusion(f32[2,12,96,128]{3,2,1,0:T(8,128)S(1)} %fusion.23, f32[2,11,96,128]{3,2,1,0:T(8,128)S(1)} %copy-done.41, f32[2,11,96,128]{3,2,1,0:T(8,128)S(1)} %fusion.36, f32[2,11,96,128]{3,2,1,0:T(8,128)S(1)} %copy-done.40, f32[2,11,96,128]{3,2,1,0:T(8,128)S(1)} %copy-done.45, ...), kind=kLoop, calls=%fused_computation.81 | loop fusion | flops 9732096 | bytes 17836480 | tf_op jit(solution)/shard_map/add | solution.py:175
  (342 shorter events, 120.0 us)
Async XLA Ops:
  0.6 34.0 %copy-start = (s32[2048]{0:T(1024)S(1)}, s32[2048]{0:T(1024)}, u32[]{:S(2)}) copy-start(s32[2048]{0:T(1024)} %param.19) | copy-start | bytes 24580
  4.6 21.0 %copy-start.85 = (f32[5,12,1,128]{3,2,1,0:T(1,128)}, f32[5,12,1,128]{3,2,1,0:T(1,128)S(1)}, u32[]{:S(2)}) copy-start(f32[5,12,1,128]{3,2,1,0:T(1,128)S(1)} %get-tuple-element.37) | copy-start | bytes 92164
  4.6 51.1 %collective-permute-start.3 = (f32[5,12,1,128]{3,2,1,0:T(1,128)}, f32[5,12,1,128]{3,2,1,0:T(1,128)}, u32[]{:S(2)}, u32[]{:S(2)}) collective-permute-start(f32[5,12,1,128]{3,2,1,0:T(1,128)} %get-tuple-element.38), channel_id=1, source_target_pairs={{0,1},{1,2},{2,3},{3,4},{4,5},{5,6},{6,7},{8,9},{9,10},{10,11},{11... | collective-permute-start | bytes 92168 | tf_op jit(solution)/shard_map/ppermute | solution.py:24
  11.3 48.5 %all-to-all-start = ((f32[16,5,12,1,128]{4,3,2,1,0:T(1,128)}), f32[16,5,12,1,128]{4,3,2,1,0:T(1,128)}, u32[]{:S(2)}, u32[]{:S(2)}) async-start(f32[16,5,12,1,128]{4,3,2,1,0:T(1,128)} %stack.26), calls=%async_computation | async-start | bytes 983040 | tf_op jit(solution)/shard_map/all_to_all | solution.py:233
  17.6 52.9 %collective-permute-start.2 = (f32[5,12,1,128]{1,0,3,2:T(8,128)}, f32[5,12,1,128]{1,0,3,2:T(8,128)}, u32[]{:S(2)}, u32[]{:S(2)}) collective-permute-start(f32[5,12,1,128]{1,0,3,2:T(8,128)} %copy.309), channel_id=1, source_target_pairs={{1,0},{2,1},{3,2},{4,3},{5,4},{6,5},{7,6},{9,8},{10,9},{11,10},{12... | collective-permute-start | bytes 92168 | tf_op jit(solution)/shard_map/ppermute | solution.py:26
  29.3 16.2 %collective-permute-start = (f32[5,12,96,1]{2,1,0,3:T(8,128)}, f32[5,12,96,1]{2,1,0,3:T(8,128)}, u32[]{:S(2)}, u32[]{:S(2)}) collective-permute-start(f32[5,12,96,1]{2,1,0,3:T(8,128)} %copy.307), channel_id=1, source_target_pairs={{8,0},{16,8},{24,16},{32,24},{40,32},{48,40},{56,48},{64,56},{72,6... | collective-permute-start | bytes 69128 | tf_op jit(solution)/shard_map/ppermute | solution.py:26
  33.4 17.8 %collective-permute-start.1 = (f32[5,12,96,1]{2,1,0,3:T(8,128)}, f32[5,12,96,1]{2,1,0,3:T(8,128)}, u32[]{:S(2)}, u32[]{:S(2)}) collective-permute-start(f32[5,12,96,1]{2,1,0,3:T(8,128)} %copy.308), channel_id=1, source_target_pairs={{0,8},{8,16},{16,24},{24,32},{32,40},{40,48},{48,56},{56,64},{64,7... | collective-permute-start | bytes 69128 | tf_op jit(solution)/shard_map/ppermute | solution.py:24
  43.4 38.5 %copy-start.12 = (f32[12,96,128]{2,1,0:T(8,128)}, f32[12,96,128]{2,1,0:T(8,128)S(1)}, u32[]{:S(2)}) copy-start(f32[12,96,128]{2,1,0:T(8,128)S(1)} %fusion.83) | copy-start | bytes 1769476
  45.5 184.7 %copy-start.100 = (pred[128]{0:T(512)(128)(4,1)}, pred[128]{0:T(512)(128)(4,1)S(1)}, u32[]{:S(2)}) copy-start(pred[128]{0:T(512)(128)(4,1)S(1)} %get-tuple-element.90) | copy-start | bytes 388
  45.5 186.9 %copy-start.98 = (pred[128]{0:T(512)(128)(4,1)}, pred[128]{0:T(512)(128)(4,1)S(1)}, u32[]{:S(2)}) copy-start(pred[128]{0:T(512)(128)(4,1)S(1)} %get-tuple-element.89) | copy-start | bytes 388
  57.9 19.1 %copy-start.5 = (f32[5,12,96,128]{3,2,1,0:T(8,128)}, f32[5,12,96,128]{3,2,1,0:T(8,128)S(1)}, u32[]{:S(2)}) copy-start(f32[5,12,96,128]{3,2,1,0:T(8,128)S(1)} %maximum_select_fusion.3) | copy-start | bytes 8847364
  78.2 17.1 %copy-start.6 = (f32[5,12,96,128]{3,2,1,0:T(8,128)}, f32[5,12,96,128]{3,2,1,0:T(8,128)S(1)}, u32[]{:S(2)}) copy-start(f32[5,12,96,128]{3,2,1,0:T(8,128)S(1)} %maximum_select_fusion.2) | copy-start | bytes 8847364
  86.9 22.6 %copy-start.16 = (f32[2,12,96,1]{3,2,1,0:T(8,128)}, f32[2,12,96,1]{3,2,1,0:T(8,128)S(1)}, u32[]{:S(2)}) copy-start(f32[2,12,96,1]{3,2,1,0:T(8,128)S(1)} %get-tuple-element.61) | copy-start | bytes 27652
  86.9 36.5 %copy-start.15 = (f32[2,12,96,1]{3,2,1,0:T(8,128)}, f32[2,12,96,1]{3,2,1,0:T(8,128)S(1)}, u32[]{:S(2)}) copy-start(f32[2,12,96,1]{3,2,1,0:T(8,128)S(1)} %get-tuple-element.60) | copy-start | bytes 27652
  91.4 24.0 %collective-permute-start.7 = (f32[2,12,1,128]{3,2,1,0:T(1,128)}, f32[2,12,1,128]{3,2,1,0:T(1,128)}, u32[]{:S(2)}, u32[]{:S(2)}) collective-permute-start(f32[2,12,1,128]{3,2,1,0:T(1,128)} %get-tuple-element.64), channel_id=1, source_target_pairs={{0,1},{1,2},{2,3},{3,4},{4,5},{5,6},{6,7},{8,9},{9,10},{10,11},{11... | collective-permute-start | bytes 36872 | tf_op jit(solution)/shard_map/ppermute | solution.py:24
  96.9 19.9 %all-to-all-start.1 = ((f32[16,2,12,1,128]{4,3,2,1,0:T(1,128)}), f32[16,2,12,1,128]{4,3,2,1,0:T(1,128)}, u32[]{:S(2)}, u32[]{:S(2)}) async-start(f32[16,2,12,1,128]{4,3,2,1,0:T(1,128)} %stack.27), calls=%async_computation.1 | async-start | bytes 393216 | tf_op jit(solution)/shard_map/all_to_all | solution.py:233
  103.4 19.3 %collective-permute-start.6 = (f32[2,12,1,128]{3,2,1,0:T(1,128)}, f32[2,12,1,128]{3,2,1,0:T(1,128)}, u32[]{:S(2)}, u32[]{:S(2)}) collective-permute-start(f32[2,12,1,128]{3,2,1,0:T(1,128)} %get-tuple-element.65), channel_id=1, source_target_pairs={{1,0},{2,1},{3,2},{4,3},{5,4},{6,5},{7,6},{9,8},{10,9},{11,10},{12... | collective-permute-start | bytes 36872 | tf_op jit(solution)/shard_map/ppermute | solution.py:26
  109.0 4.5 %collective-permute-start.4 = (f32[2,12,96,1]{2,0,3,1:T(2,128)}, f32[2,12,96,1]{2,0,3,1:T(2,128)}, u32[]{:S(2)}, u32[]{:S(2)}) collective-permute-start(f32[2,12,96,1]{2,0,3,1:T(2,128)} %copy.250), channel_id=1, source_target_pairs={{8,0},{16,8},{24,16},{32,24},{40,32},{48,40},{56,48},{64,56},{72,6... | collective-permute-start | bytes 27656 | tf_op jit(solution)/shard_map/ppermute | solution.py:26
  110.5 4.4 %collective-permute-start.5 = (f32[2,12,96,1]{2,0,3,1:T(2,128)}, f32[2,12,96,1]{2,0,3,1:T(2,128)S(1)}, u32[]{:S(2)}, u32[]{:S(2)}) collective-permute-start(f32[2,12,96,1]{2,0,3,1:T(2,128)} %copy.252), channel_id=1, source_target_pairs={{0,8},{8,16},{16,24},{24,32},{32,40},{40,48},{48,56},{56,64},{64,7... | collective-permute-start | bytes 27656 | tf_op jit(solution)/shard_map/ppermute | solution.py:24
  123.5 10.5 %copy-start.17 = (f32[2,12,96,1]{3,2,1,0:T(8,128)S(1)}, f32[2,12,96,1]{3,2,1,0:T(8,128)}, u32[]{:S(2)}) copy-start(f32[2,12,96,1]{3,2,1,0:T(8,128)} %copy-done.16) | copy-start | bytes 27652
  123.5 10.5 %copy-start.36 = (f32[2,12,96,127]{3,2,1,0:T(8,128)S(1)}, f32[2,12,96,127]{3,2,1,0:T(8,128)}, u32[]{:S(2)}) copy-start(f32[2,12,96,127]{3,2,1,0:T(8,128)} %get-tuple-element.58) | copy-start | bytes 3511300
  138.2 45.2 %copy-start.2 = (f32[2,12,96,128]{3,2,1,0:T(8,128)}, f32[2,12,96,128]{3,2,1,0:T(8,128)S(1)}, u32[]{:S(2)}) copy-start(f32[2,12,96,128]{3,2,1,0:T(8,128)S(1)} %fusion.18) | copy-start | bytes 3538948
  149.0 25.4 %collective-permute-start.8 = (f32[4,12,96,1]{2,0,3,1:T(4,128)}, f32[4,12,96,1]{2,0,3,1:T(4,128)}, u32[]{:S(2)}, u32[]{:S(2)}) collective-permute-start(f32[4,12,96,1]{2,0,3,1:T(4,128)} %copy.310), channel_id=1, source_target_pairs={{8,0},{16,8},{24,16},{32,24},{40,32},{48,40},{56,48},{64,56},{72,6... | collective-permute-start | bytes 55304 | tf_op jit(solution)/shard_map/ppermute | solution.py:26
  155.8 19.3 %collective-permute-start.9 = (f32[4,12,96,1]{2,0,3,1:T(4,128)}, f32[4,12,96,1]{2,0,3,1:T(4,128)}, u32[]{:S(2)}, u32[]{:S(2)}) collective-permute-start(f32[4,12,96,1]{2,0,3,1:T(4,128)} %copy.311), channel_id=1, source_target_pairs={{0,8},{8,16},{16,24},{24,32},{32,40},{40,48},{48,56},{56,64},{64,7... | collective-permute-start | bytes 55304 | tf_op jit(solution)/shard_map/ppermute | solution.py:24
  157.3 25.4 %collective-permute-start.11 = (f32[4,12,1,128]{3,2,1,0:T(1,128)}, f32[4,12,1,128]{3,2,1,0:T(1,128)}, u32[]{:S(2)}, u32[]{:S(2)}) collective-permute-start(f32[4,12,1,128]{3,2,1,0:T(1,128)} %get-tuple-element.44), channel_id=1, source_target_pairs={{0,1},{1,2},{2,3},{3,4},{4,5},{5,6},{6,7},{8,9},{9,10},{10,11},{11... | collective-permute-start | bytes 73736 | tf_op jit(solution)/shard_map/ppermute | solution.py:24
  161.3 24.9 %all-to-all-start.2 = ((f32[16,4,12,1,128]{4,1,2,3,0:T(4,128)}), f32[16,4,12,1,128]{4,1,2,3,0:T(4,128)}, u32[]{:S(2)}, u32[]{:S(2)}) async-start(f32[16,4,12,1,128]{4,1,2,3,0:T(4,128)} %stack.28), calls=%async_computation.2 | async-start | bytes 786432 | tf_op jit(solution)/shard_map/all_to_all | solution.py:233
  168.7 25.1 %collective-permute-start.10 = (f32[4,12,1,128]{3,0,1,2:T(4,128)}, f32[4,12,1,128]{3,0,1,2:T(4,128)}, u32[]{:S(2)}, u32[]{:S(2)}) collective-permute-start(f32[4,12,1,128]{3,0,1,2:T(4,128)} %copy.312), channel_id=1, source_target_pairs={{1,0},{2,1},{3,2},{4,3},{5,4},{6,5},{7,6},{9,8},{10,9},{11,10},{12... | collective-permute-start | bytes 73736 | tf_op jit(solution)/shard_map/ppermute | solution.py:26
  206.8 22.1 %collective-permute-start.12 = (f32[2,12,96,1]{2,0,3,1:T(2,128)}, f32[2,12,96,1]{2,0,3,1:T(2,128)}, u32[]{:S(2)}, u32[]{:S(2)}) collective-permute-start(f32[2,12,96,1]{2,0,3,1:T(2,128)} %copy.280), channel_id=1, source_target_pairs={{8,0},{16,8},{24,16},{32,24},{40,32},{48,40},{56,48},{64,56},{72,6... | collective-permute-start | bytes 27656 | tf_op jit(solution)/shard_map/ppermute | solution.py:26
  210.4 19.1 %collective-permute-start.13 = (f32[2,12,96,1]{2,0,3,1:T(2,128)}, f32[2,12,96,1]{2,0,3,1:T(2,128)}, u32[]{:S(2)}, u32[]{:S(2)}) collective-permute-start(f32[2,12,96,1]{2,0,3,1:T(2,128)} %copy.282), channel_id=1, source_target_pairs={{0,8},{8,16},{16,24},{24,32},{32,40},{40,48},{48,56},{56,64},{64,7... | collective-permute-start | bytes 27656 | tf_op jit(solution)/shard_map/ppermute | solution.py:24
  212.3 26.5 %collective-permute-start.15 = (f32[2,12,1,128]{3,2,1,0:T(1,128)}, f32[2,12,1,128]{3,2,1,0:T(1,128)}, u32[]{:S(2)}, u32[]{:S(2)}) collective-permute-start(f32[2,12,1,128]{3,2,1,0:T(1,128)} %get-tuple-element.57), channel_id=1, source_target_pairs={{0,1},{1,2},{2,3},{3,4},{4,5},{5,6},{6,7},{8,9},{9,10},{10,11},{11... | collective-permute-start | bytes 36872 | tf_op jit(solution)/shard_map/ppermute | solution.py:24
  215.8 27.0 %all-to-all-start.3 = ((f32[16,2,12,1,128]{4,3,2,1,0:T(1,128)}), f32[16,2,12,1,128]{4,3,2,1,0:T(1,128)}, u32[]{:S(2)}, u32[]{:S(2)}) async-start(f32[16,2,12,1,128]{4,3,2,1,0:T(1,128)} %stack.29), calls=%async_computation.3 | async-start | bytes 393216 | tf_op jit(solution)/shard_map/all_to_all | solution.py:233
  222.4 30.3 %collective-permute-start.14 = (f32[2,12,1,128]{3,2,1,0:T(1,128)}, f32[2,12,1,128]{3,2,1,0:T(1,128)}, u32[]{:S(2)}, u32[]{:S(2)}) collective-permute-start(f32[2,12,1,128]{3,2,1,0:T(1,128)} %get-tuple-element.56), channel_id=1, source_target_pairs={{1,0},{2,1},{3,2},{4,3},{5,4},{6,5},{7,6},{9,8},{10,9},{11,10},{12... | collective-permute-start | bytes 36872 | tf_op jit(solution)/shard_map/ppermute | solution.py:26
  (93 other events, 376.5 us)
